TPU v7x, 256 devices: a whole 4x4x8 slice. The times are simulated.
256 devices in a mesh: dp: 4 (over y_hi, core), expert: 64 (over x, z, y_lo).
Axes of the slice: x: 4, y: 4 (y_hi: 2, y_lo: 2; y = y_hi * 2 + y_lo), z: 8, core: 2. Of those that a mesh axis runs over, the one named last changes fastest.
Arguments:
- tokens: bfloat16 [4, 8192, 3584], P('dp', 'expert'), may hold values from -6 to 6
- cotangent: bfloat16 [4, 8192, 1024], P('dp', 'expert'), may hold values from -12 to 12
- gate_weights: float32 [4, 8192], replicated, may hold values from 0.1 to 1
- tile_expert: int32 [4, 64], replicated, may hold values from 0 to 63, as said below
- w_gate: bfloat16 [64, 3584, 1024], P('expert', None, 'dp'), may hold values from -0.09375 to 0.09375
- w_up: bfloat16 [64, 3584, 1024], P('expert', None, 'dp'), may hold values from -0.09375 to 0.09375
Outputs:
- d_tokens: bfloat16 [4, 8192, 3584], P('dp', 'expert')
- hidden: bfloat16 [4, 8192, 1024], P(None, 'expert', 'dp')
- grad_gate: bfloat16 [64, 3584, 1024], P('expert', None, 'dp')
- grad_up: bfloat16 [64, 3584, 1024], P('expert', None, 'dp')
Inputs may be any that keep to these rules, and one draw needn't show every extreme that they name: tile_expert[g, j] is either j or (j + 1) mod 64: the expert of the tile's own index of the expert axis or of the next index round the closed cycle.
All inputs are finite; a program needn't handle non-finite values.
Results may differ from a plain program's by a relative error of at most 0.009.
Values may be sent and summed in bfloat16 or wider, within the bound.
A program may use at most 128 MiB of HBM per device.

v0:
```python
import jax
import jax.numpy as jnp
from jax import lax
from jax.sharding import Mesh
from jax.sharding import PartitionSpec as P

TILE = 128
DP = ("dp_0", "dp_1")


def in_blocks(x, dim, count):
    before, after = (x.shape[:dim], x.shape[dim + 1 :])
    return jnp.moveaxis(x.reshape(*before, count, -1, *after), dim, 0)


def joined_along(pieces, dim):
    dims = list(pieces.shape[1:])
    dims[dim] *= pieces.shape[0]
    return jnp.moveaxis(pieces, 0, dim).reshape(dims)


def exchange_in_order(pieces, axes, order):
    inside = pieces.shape[1:]
    out = pieces.reshape(*(lax.axis_size(a) for a in axes), *inside)
    for k in order:
        out = lax.all_to_all(out, axes[k], k, k, tiled=True)
    return out.reshape(-1, *inside)


def core_and_chips(x, groups, order, split_dim, concat_dim):
    count = lax.axis_size(groups[0]) * lax.axis_size(groups[1])
    pieces = in_blocks(x, split_dim, count)
    return joined_along(exchange_in_order(pieces, groups, order), concat_dim)


def shifted(value, axis, steps):
    count = lax.axis_size(axis)
    pairs = [(source, (source + steps) % count) for source in range(count)]
    return lax.ppermute(value, axis, pairs)


def sent_and_summed(x, axis, dim):
    count = lax.axis_size(axis)
    pieces = lax.all_to_all(in_blocks(x, dim, count), axis, 0, 0, tiled=True)
    return jnp.sum(pieces.astype(jnp.float32), axis=0)


def contract(left, right, left_axis, right_axis):
    return lax.dot_general(
        left, right, (((left_axis,), (right_axis,)), ((), ())), preferred_element_type=jnp.float32
    )


def route_scale(tile_expert, gate_weights, source, expert, row_count):
    tile_count = row_count // TILE
    owners = lax.dynamic_slice_in_dim(tile_expert, source * tile_count, tile_count, 1)
    weights = lax.dynamic_slice_in_dim(gate_weights, source * row_count, row_count, 1)
    routed = jnp.repeat(owners == expert, TILE, axis=1, total_repeat_length=row_count)
    return jnp.where(routed, weights, jnp.zeros_like(weights))


def expert_pass(cand_rows, cand_grads, row_scale, gate_panel, up_panel):
    groups, row_total, model_width = cand_rows.shape
    quarter = gate_panel.shape[1]
    flat_rows = cand_rows.reshape(groups * row_total, model_width)
    gate_val = jnp.dot(flat_rows, gate_panel, preferred_element_type=jnp.float32)
    up_val = jnp.dot(flat_rows, up_panel, preferred_element_type=jnp.float32)
    sigmoid_val = jax.nn.sigmoid(gate_val)
    activation = gate_val * sigmoid_val
    factor = row_scale.reshape(groups * row_total, 1)
    hidden_part = (factor * activation * up_val).astype(jnp.bfloat16)
    act_grad = factor * cand_grads.reshape(groups * row_total, quarter).astype(jnp.float32)
    up_grad = (act_grad * activation).astype(jnp.bfloat16)
    gate_grad = (act_grad * up_val * sigmoid_val * (1.0 + gate_val * (1.0 - sigmoid_val))).astype(
        jnp.bfloat16
    )
    partial_value = (
        contract(gate_grad, gate_panel, 1, 1) + contract(up_grad, up_panel, 1, 1)
    ).astype(jnp.bfloat16)
    partial_value = lax.optimization_barrier(partial_value)
    grad_gate = contract(flat_rows, gate_grad, 0, 0)
    grad_up = contract(flat_rows, up_grad, 0, 0)
    return (
        partial_value.reshape(groups, row_total, model_width),
        hidden_part.reshape(groups, row_total, quarter),
        grad_gate,
        grad_up,
    )


def to_groups(tile_rows, tile_grads):
    gathered = lax.all_gather(tile_rows, DP, axis=0, tiled=True)
    quarters = core_and_chips(tile_grads, ("dp_0", "dp_1"), (1, 0), 2, 0)
    return (gathered, quarters)


def cycle_ahead(tile_rows, tile_grads):
    return shifted((tile_rows, tile_grads), "expert", 1)


def cycle_return(row_sums, hidden_part):
    return shifted((row_sums, hidden_part), "expert", -1)


def quarter_total(terms):
    return sent_and_summed(terms.astype(jnp.bfloat16), DP, 0)


def per_device(tokens, cotangent, gate_weights, tile_expert, w_gate, w_up):
    row_count = tokens.shape[1]
    cycle_size = lax.axis_size("expert")
    position = lax.axis_index("expert")
    prev_place = (position + cycle_size - 1) % cycle_size
    gate_panel = w_gate[0]
    up_panel = w_up[0]
    own_scale = route_scale(tile_expert, gate_weights, position, position, row_count)
    prev_scale = route_scale(tile_expert, gate_weights, prev_place, position, row_count)
    near_rows, near_grads = cycle_ahead(tokens, cotangent)
    cand_rows, cand_grads = to_groups(
        jnp.concatenate([tokens, near_rows], 1), jnp.concatenate([cotangent, near_grads], 1)
    )
    row_scale = jnp.concatenate([own_scale, prev_scale], 1)
    partial_value, hidden_part, grad_gate, grad_up = expert_pass(
        cand_rows, cand_grads, row_scale, gate_panel, up_panel
    )
    summed = quarter_total(partial_value.astype(jnp.float32)).astype(jnp.bfloat16)
    back_rows, back_hidden = cycle_return(summed[:, row_count:], hidden_part[:, row_count:])
    d_tokens = (summed[:, :row_count].astype(jnp.float32) + back_rows.astype(jnp.float32)).astype(
        jnp.bfloat16
    )
    hidden = (
        hidden_part[:, :row_count].astype(jnp.float32) + back_hidden.astype(jnp.float32)
    ).astype(jnp.bfloat16)
    grad_gate = (grad_gate / TILE).astype(jnp.bfloat16)[None]
    grad_up = (grad_up / TILE).astype(jnp.bfloat16)[None]
    return (d_tokens, hidden, grad_gate, grad_up)


def solution(mesh):
    split = Mesh(mesh.devices.reshape(2, 2, mesh.shape["expert"]), ("dp_0", "dp_1", "expert"))
    placed = (
        P(DP, "expert", None),
        P(DP, "expert", None),
        P(),
        P(),
        P("expert", None, DP),
        P("expert", None, DP),
    )
    return jax.shard_map(
        per_device,
        mesh=split,
        in_specs=placed,
        out_specs=(
            P(DP, "expert", None),
            P(None, "expert", DP),
            P("expert", None, DP),
            P("expert", None, DP),
        ),
        check_vma=False,
    )
```

profile of v0, /device:TPU:2, one launch (start us, length us, event | category | flops | bytes accessed | tf_op | source)
XLA Modules:
  0.0 264.4 jit_solution(17189211925136848051)
XLA Ops:
  7.2 0.0 copy-start
  7.2 0.0 copy-start.4
  7.2 0.0 copy-start.5
  7.2 0.0 all-gather.2.cloned.1.call-start
  7.2 1.7 collective-permute-start.1
  8.9 25.8 %collective-permute-done.1 = bf16[1,128,3584]{2,1,0:T(8,128)(2,1)S(1)} collective-permute-done((bf16[1,128,3584]{2,1,0:T(8,128)(2,1)}, bf16[1,128,3584]{2,1,0:T(8,128)(2,1)S(1)}, u32[]{:S(2)}, u32[]{:S(2)}) %collective-permute-start.1) | collective-permute-done | bytes 917536 | tf_op jit(solution)/shard_map/ppermute | solution.py:39
  34.7 2.5 pad_maximum_fusion
  37.2 0.0 all-gather.2.cloned.1.call-update
  37.3 0.0 copy-done.4
  37.3 0.2 copy.17
  37.5 0.1 collective-permute-start
  37.6 0.0 copy-done.5
  37.6 0.2 fusion.18
  37.8 0.8 dynamic-slice_select_fusion.1
  38.6 9.4 %collective-permute-done = bf16[1,128,1024]{1,2,0:T(8,128)(2,1)S(1)} collective-permute-done((bf16[1,128,1024]{1,2,0:T(8,128)(2,1)S(1)}, bf16[1,128,1024]{1,2,0:T(8,128)(2,1)S(1)}, u32[]{:S(2)}, u32[]{:S(2)}) %collective-permute-start) | collective-permute-done | bytes 262176 | tf_op jit(solution)/shard_map/ppermute | solution.py:39
  48.0 0.1 pad_maximum_fusion.1
  48.1 0.2 copy.19
  48.3 4.5 %all_to_all.15 = bf16[2,2,1,256,256]{4,3,0,2,1:T(8,128)(2,1)S(1)} all-to-all(bf16[2,2,1,256,256]{4,3,0,2,1:T(8,128)(2,1)S(1)} %copy.19), channel_id=1, replica_groups=mesh['dp_0'=2,'dp_1'=2,'expert'=64] {'dp_1'}, dimensions={1} | all-to-all | bytes 1048576 | tf_op jit(solution)/shard_map/all_to_all | solution.py:26
  52.7 0.8 copy.20
  53.6 4.2 %all-to-all-start.1 = ((bf16[2,2,1,256,256]{4,3,1,2,0:T(8,128)(2,1)}), bf16[2,2,1,256,256]{4,3,1,2,0:T(8,128)(2,1)S(1)}, u32[]{:S(2)}, u32[]{:S(2)}) async-start(bf16[2,2,1,256,256]{4,3,1,2,0:T(8,128)(2,1)} %copy.20), calls=%async_computation.1 | async-start | bytes 1048576 | tf_op jit(solution)/shard_map/all_to_all | solution.py:26
  57.7 44.2 %all-gather.2.cloned.1.call-done = bf16[4,256,3584]{2,1,0:T(8,128)(2,1)} async-done(((bf16[1,256,3584]{2,1,0:T(8,128)(2,1)}), bf16[4,256,3584]{2,1,0:T(8,128)(2,1)}) %all-gather.2.cloned.1.call-update) | async-done | bytes 7340048 | tf_op jit(solution)/shard_map/all_gather | solution.py:92
  101.9 6.6 %fusion.6 = f32[1024,256]{1,0:T(8,128)} fusion(bf16[1024,3584]{1,0:T(8,128)(2,1)} %bitcast.49, bf16[1,3584,256]{2,1,0:T(8,128)(2,1)} %param.20), kind=kOutput, calls=%fused_computation.10 | convolution fusion | flops 1879048192 | bytes 10223616 | tf_op jit(solution)/shard_map/dot_general | solution.py:66
  108.5 0.0 all-to-all-done.1
  108.5 0.0 copy-start.3
  108.5 0.8 copy-done.3
  109.3 0.0 copy-done
  109.3 0.0 copy-start.2
  109.3 5.9 %multiply_convert_fusion = (bf16[1024,256]{1,0:T(8,128)(2,1)S(1)}, bf16[1024,256]{1,0:T(8,128)(2,1)S(1)}, bf16[1024,256]{1,0:T(8,128)(2,1)S(1)}) fusion(f32[1024]{0:T(1024)S(1)} %bitcast.48, f32[1024,256]{1,0:T(8,128)} %fusion.6, bf16[2,2,1,256,256]{4,3,1,2,0:T(8,128)(2,1)} %copy-done.3, bf16[1024,3584]{1,0:T(8,128)(2,1)} %bitcast.50, ...), kind=kOutput, calls=%fused_computation.23 | convolution fusion | flops 1883766784 | bytes 12324864 | tf_op jit(solution)/shard_map/dot_general | solution.py:67
  115.3 0.0 copy-done.2
  115.3 7.3 %fusion.4 = f32[1024,3584]{1,0:T(8,128)} fusion(bf16[1024,256]{1,0:T(8,128)(2,1)S(1)} %get-tuple-element.48, bf16[1,3584,256]{2,1,0:T(8,128)(2,1)S(1)} %copy-done.2), kind=kOutput, calls=%fused_computation.8 | convolution fusion | flops 1879048192 | bytes 17039360 | tf_op jit(solution)/shard_map/dot_general | solution.py:49
  122.6 10.2 %add_convert_fusion = bf16[1024,3584]{1,0:T(8,128)(2,1)} fusion(f32[1024,3584]{1,0:T(8,128)} %fusion.4, bf16[1024,256]{1,0:T(8,128)(2,1)S(1)} %get-tuple-element.49, bf16[1,3584,256]{2,1,0:T(8,128)(2,1)S(1)} %copy-done), kind=kOutput, calls=%fused_computation | convolution fusion | flops 1886388224 | bytes 24379392 | tf_op jit(solution)/shard_map/dot_general | solution.py:49
  132.8 5.4 %all-to-all-start.2 = ((bf16[4,1,256,3584]{3,2,1,0:T(8,128)(2,1)}), bf16[4,1,256,3584]{3,2,1,0:T(8,128)(2,1)}, u32[]{:S(2)}, u32[]{:S(2)}) async-start(bf16[4,1,256,3584]{3,2,1,0:T(8,128)(2,1)} %bitcast.42), calls=%async_computation.2 | async-start | bytes 14680064 | tf_op jit(solution)/shard_map/all_to_all | solution.py:44
  138.3 0.7 slice.47
  139.0 3.3 %collective-permute-start.3 = (bf16[4,128,256]{2,1,0:T(8,128)(2,1)}, bf16[4,128,256]{2,1,0:T(8,128)(2,1)}, u32[]{:S(2)}, u32[]{:S(2)}) collective-permute-start(bf16[4,128,256]{2,1,0:T(8,128)(2,1)} %slice.47), channel_id=1, source_target_pairs={{0,63},{1,0},{2,1},{3,2},{4,3},{5,4},{6,5},{7,6},{8,7},{9,8},{10,9... | collective-permute-start | bytes 786440 | tf_op jit(solution)/shard_map/ppermute | solution.py:39
  142.3 6.4 %fusion.3 = bf16[1,3584,256]{2,1,0:T(8,128)(2,1)} fusion(bf16[1024,3584]{1,0:T(8,128)(2,1)} %bitcast.51, bf16[1024,256]{1,0:T(8,128)(2,1)S(1)} %get-tuple-element.48), kind=kOutput, calls=%fused_computation.6 | convolution fusion | flops 1880883200 | bytes 9699328 | tf_op jit(solution)/shard_map/dot_general | solution.py:49
  148.8 78.5 %all-to-all-done.2 = bf16[4,1,256,3584]{3,2,1,0:T(8,128)(2,1)} async-done(((bf16[4,1,256,3584]{3,2,1,0:T(8,128)(2,1)}), bf16[4,1,256,3584]{3,2,1,0:T(8,128)(2,1)}, u32[]{:S(2)}, u32[]{:S(2)}) %all-to-all-start.2) | async-done | bytes 7340064 | tf_op jit(solution)/shard_map/all_to_all | solution.py:44
  227.3 6.0 %reduce_sum.14 = bf16[256,3584]{1,0:T(8,128)(2,1)} reduce(bf16[4,1,256,3584]{3,2,1,0:T(8,128)(2,1)} %all-to-all-done.2, bf16[]{:T(256)} %constant.151.clone.1), dimensions={0,1}, to_apply=%region_0.2 | reduce | flops 2752512 | bytes 9175042 | tf_op jit(solution)/shard_map/reduce_sum | solution.py:45
  233.3 1.2 slice.45
  234.6 0.0 copy-start.1
  234.6 0.1 collective-permute-start.2
  234.7 6.6 %fusion.2 = bf16[1,3584,256]{2,1,0:T(8,128)(2,1)} fusion(bf16[1024,3584]{1,0:T(8,128)(2,1)} %bitcast.52, bf16[1024,256]{1,0:T(8,128)(2,1)S(1)} %get-tuple-element.49), kind=kOutput, calls=%fused_computation.5 | convolution fusion | flops 1880883200 | bytes 9699328 | tf_op jit(solution)/shard_map/dot_general | solution.py:49
  241.2 0.0 collective-permute-done.3
  241.2 1.7 add_convert_fusion.2
  243.0 13.5 %collective-permute-done.2 = bf16[1,128,3584]{2,1,0:T(8,128)(2,1)S(1)} collective-permute-done((bf16[1,128,3584]{2,1,0:T(8,128)(2,1)S(1)}, bf16[1,128,3584]{2,1,0:T(8,128)(2,1)S(1)}, u32[]{:S(2)}, u32[]{:S(2)}) %collective-permute-start.2) | collective-permute-done | bytes 917536 | tf_op jit(solution)/shard_map/ppermute | solution.py:39
  256.5 0.0 copy-done.1
  256.5 1.1 add_convert_fusion.1
  (2 shorter events, 0.0 us)
Async XLA Ops:
  7.2 102.2 %copy-start = (bf16[1,3584,256]{2,1,0:T(8,128)(2,1)S(1)}, bf16[1,3584,256]{2,1,0:T(8,128)(2,1)}, u32[]{:S(2)}) copy-start(bf16[1,3584,256]{2,1,0:T(8,128)(2,1)} %param.21) | copy-start | bytes 5505028
  7.2 30.1 %copy-start.4 = (bf16[1,128,1024]{2,1,0:T(8,128)(2,1)S(1)}, bf16[1,128,1024]{2,1,0:T(8,128)(2,1)}, u32[]{:S(2)}) copy-start(bf16[1,128,1024]{2,1,0:T(8,128)(2,1)} %param.17) | copy-start | bytes 786436
  7.2 30.4 %copy-start.5 = (s32[4,64]{1,0:T(4,128)S(1)}, s32[4,64]{1,0:T(4,128)}, u32[]{:S(2)}) copy-start(s32[4,64]{1,0:T(4,128)} %param.19) | copy-start | bytes 3076
  7.2 94.7 %all-gather.2.cloned.1.call-start = ((), (), s32[]{:S(2)}) async-start(), calls=%async_computation.3 | async-start | bytes 9175040 | tf_op jit(solution)/shard_map/all_gather | solution.py:92
  7.2 27.5 %collective-permute-start.1 = (bf16[1,128,3584]{2,1,0:T(8,128)(2,1)}, bf16[1,128,3584]{2,1,0:T(8,128)(2,1)S(1)}, u32[]{:S(2)}, u32[]{:S(2)}) collective-permute-start(bf16[1,128,3584]{2,1,0:T(8,128)(2,1)} %param.16), channel_id=1, source_target_pairs={{0,1},{1,2},{2,3},{3,4},{4,5},{5,6},{6,7},{7,8},{8,9},{9,10},{10,1... | collective-permute-start | bytes 2752520 | tf_op jit(solution)/shard_map/ppermute | solution.py:39
  37.5 10.6 %collective-permute-start = (bf16[1,128,1024]{1,2,0:T(8,128)(2,1)S(1)}, bf16[1,128,1024]{1,2,0:T(8,128)(2,1)S(1)}, u32[]{:S(2)}, u32[]{:S(2)}) collective-permute-start(bf16[1,128,1024]{1,2,0:T(8,128)(2,1)S(1)} %copy.17), channel_id=1, source_target_pairs={{0,1},{1,2},{2,3},{3,4},{4,5},{5,6},{6,7},{7,8},{8,9},{9,10},{10,1... | collective-permute-start | bytes 786440 | tf_op jit(solution)/shard_map/ppermute | solution.py:39
  53.6 55.0 %all-to-all-start.1 = ((bf16[2,2,1,256,256]{4,3,1,2,0:T(8,128)(2,1)}), bf16[2,2,1,256,256]{4,3,1,2,0:T(8,128)(2,1)S(1)}, u32[]{:S(2)}, u32[]{:S(2)}) async-start(bf16[2,2,1,256,256]{4,3,1,2,0:T(8,128)(2,1)} %copy.20), calls=%async_computation.1 | async-start | bytes 1048576 | tf_op jit(solution)/shard_map/all_to_all | solution.py:26
  108.5 0.8 copy-start.3
  109.3 5.9 %copy-start.2 = (bf16[1,3584,256]{2,1,0:T(8,128)(2,1)S(1)}, bf16[1,3584,256]{2,1,0:T(8,128)(2,1)}, u32[]{:S(2)}) copy-start(bf16[1,3584,256]{2,1,0:T(8,128)(2,1)} %param.20) | copy-start | bytes 5505028
  132.8 94.5 %all-to-all-start.2 = ((bf16[4,1,256,3584]{3,2,1,0:T(8,128)(2,1)}), bf16[4,1,256,3584]{3,2,1,0:T(8,128)(2,1)}, u32[]{:S(2)}, u32[]{:S(2)}) async-start(bf16[4,1,256,3584]{3,2,1,0:T(8,128)(2,1)} %bitcast.42), calls=%async_computation.2 | async-start | bytes 14680064 | tf_op jit(solution)/shard_map/all_to_all | solution.py:44
  139.0 102.2 %collective-permute-start.3 = (bf16[4,128,256]{2,1,0:T(8,128)(2,1)}, bf16[4,128,256]{2,1,0:T(8,128)(2,1)}, u32[]{:S(2)}, u32[]{:S(2)}) collective-permute-start(bf16[4,128,256]{2,1,0:T(8,128)(2,1)} %slice.47), channel_id=1, source_target_pairs={{0,63},{1,0},{2,1},{3,2},{4,3},{5,4},{6,5},{7,6},{8,7},{9,8},{10,9... | collective-permute-start | bytes 786440 | tf_op jit(solution)/shard_map/ppermute | solution.py:39
  234.6 21.9 %copy-start.1 = (bf16[256,3584]{1,0:T(8,128)(2,1)S(1)}, bf16[256,3584]{1,0:T(8,128)(2,1)}, u32[]{:S(2)}) copy-start(bf16[256,3584]{1,0:T(8,128)(2,1)} %reduce_sum.14) | copy-start | bytes 5505028
  234.6 21.9 %collective-permute-start.2 = (bf16[1,128,3584]{2,1,0:T(8,128)(2,1)S(1)}, bf16[1,128,3584]{2,1,0:T(8,128)(2,1)S(1)}, u32[]{:S(2)}, u32[]{:S(2)}) collective-permute-start(bf16[1,128,3584]{2,1,0:T(8,128)(2,1)S(1)} %slice.45), channel_id=1, source_target_pairs={{0,63},{1,0},{2,1},{3,2},{4,3},{5,4},{6,5},{7,6},{8,7},{9,8},{10,9... | collective-permute-start | bytes 2752520 | tf_op jit(solution)/shard_map/ppermute | solution.py:39
Sparse Core Ops, SparseCore 0:
  37.4 64.4 all-gather.1
where the time goes:
time: 265 us; the launch traced here: 264 us
  waiting for transfers between devices  172 us (65%)
  matrix products  43.1 us (16%)
  starting transfers between devices  14.8 us (6%)
  between operations  14.2 us (5%)
  other arithmetic  12.4 us (5%)
  blocking collectives  4.45 us (2%)
  local copies, waits for them, and re-layouts  3.98 us (2%)
    all_to_all x1, waiting for transfers between devices, sent_and_summed(): pieces = lax.all_to_all(in_blocks(x, dim, count), axis, 0, 0, tiled=True)  78.5 us
    ppermute x4, waiting for transfers between devices, shifted(): return lax.ppermute(value, axis, pairs)  48.7 us
    all_gather x1, waiting for transfers between devices, to_groups(): gathered = lax.all_gather(tile_rows, DP, axis=0, tiled=True)  44.2 us
    dot_general x4, matrix products, contract(): lax.dot_general(left, right, (((left_axis,), (right_axis,)), ((), ())), p...  30.5 us
    dot_general x1, matrix products, expert_pass(): jnp.dot(flat_rows, gate_panel, preferred_element_type=jnp.float32)  6.61 us
    reduce_sum x1, other arithmetic, sent_and_summed(): return jnp.sum(pieces.astype(jnp.float32), axis=0)  6.01 us
    dot_general x1, matrix products, expert_pass(): up_val = jnp.dot(flat_rows, up_panel, preferred_element_type=jnp.float32)  5.93 us
    all_to_all x1, starting transfers between devices, sent_and_summed(): pieces = lax.all_to_all(in_blocks(x, dim, count), axis, 0, 0, tiled=True)  5.45 us
  transfers between devices with their start and end apart: 7, of which 5 were waited for; matrix products, arithmetic and copies ran while one was open for 12% of the time, Pallas kernels for 0%

commit v1 on v0

--- a/solution.py
+++ b/solution.py
@@ -6,6 +6,13 @@
 
 TILE = 128
 DP = ("dp_0", "dp_1")
+
+
+def all_by_exchange(x, axis, dim):
+    size = lax.axis_size(axis)
+    shards = jnp.stack([x for _ in range(size)])
+    shards = lax.all_to_all(shards, axis, split_axis=0, concat_axis=0)
+    return jnp.concatenate(shards, axis=dim)
 
 
 def in_blocks(x, dim, count):
@@ -89,7 +96,7 @@
 
 
 def to_groups(tile_rows, tile_grads):
-    gathered = lax.all_gather(tile_rows, DP, axis=0, tiled=True)
+    gathered = all_by_exchange(tile_rows, DP, 0)
     quarters = core_and_chips(tile_grads, ("dp_0", "dp_1"), (1, 0), 2, 0)
     return (gathered, quarters)
 

time: 265 us -> 297 us (1.12)
  waiting for transfers between devices: 172 us -> 205 us
  between operations: 14.2 us -> 0.78 us
  starting transfers between devices: 14.8 us -> 23.4 us
  local copies, waits for them, and re-layouts: 3.98 us -> 10.7 us
  blocking collectives: 4.45 us -> 0 us
    all_to_all x0 -> x1, waiting for transfers between devices: none -> 81.5 us  [all_by_exchange(): shards = lax.all_to_all(shards, axis, split_axis=0, concat_axis=0)]
    all_gather x1 -> x0, waiting for transfers between devices: 44.2 us -> none  [to_groups(): gathered = lax.all_gather(tile_rows, DP, axis=0, tiled=True)]
    ppermute x4, waiting for transfers between devices: 48.7 us -> 42.5 us  [shifted(): return lax.ppermute(value, axis, pairs)]
    all_to_all x0 -> x1, starting transfers between devices: none -> 5.59 us  [all_by_exchange(): shards = lax.all_to_all(shards, axis, split_axis=0, concat_axis=0)]
    another operation x0 -> x1, local copies, waits for them, and re-layouts: none -> 5 us  [all_by_exchange(): shards = jnp.stack([x for _ in range(size)])]
    all_to_all x1 -> x0, blocking collectives: 4.45 us -> none  [exchange_in_order(): out = lax.all_to_all(out, axes[k], k, k, tiled=True)]
    all_to_all x1 -> x2, starting transfers between devices: 4.16 us -> 6.98 us  [exchange_in_order(): out = lax.all_to_all(out, axes[k], k, k, tiled=True)]
  transfers between devices with their start and end apart: 7 -> 8, of which waited for: 5 -> 5; matrix products, arithmetic and copies ran while one was open for 12% -> 12% of each run, Pallas kernels for 0% -> 0%
where the time goes in v1:
time: 297 us; the launch traced here: 296 us
  waiting for transfers between devices  205 us (69%)
  matrix products  43.1 us (15%)
  starting transfers between devices  23.4 us (8%)
  other arithmetic  12.5 us (4%)
  local copies, waits for them, and re-layouts  10.7 us (4%)
    all_to_all x1, waiting for transfers between devices, all_by_exchange(): shards = lax.all_to_all(shards, axis, split_axis=0, concat_axis=0)  81.5 us
    all_to_all x1, waiting for transfers between devices, sent_and_summed(): pieces = lax.all_to_all(in_blocks(x, dim, count), axis, 0, 0, tiled=True)  78.5 us
    ppermute x4, waiting for transfers between devices, shifted(): return lax.ppermute(value, axis, pairs)  42.5 us
    dot_general x4, matrix products, contract(): lax.dot_general(left, right, (((left_axis,), (right_axis,)), ((), ())), p...  30.5 us
    all_to_all x2, starting transfers between devices, exchange_in_order(): out = lax.all_to_all(out, axes[k], k, k, tiled=True)  6.98 us
    dot_general x1, matrix products, expert_pass(): jnp.dot(flat_rows, gate_panel, preferred_element_type=jnp.float32)  6.61 us
    reduce_sum x1, other arithmetic, sent_and_summed(): return jnp.sum(pieces.astype(jnp.float32), axis=0)  6 us
  transfers between devices with their start and end apart: 8, of which 5 were waited for; matrix products, arithmetic and copies ran while one was open for 12% of the time, Pallas kernels for 0%

profile of v1, /device:TPU:2, one launch (start us, length us, event | category | flops | bytes accessed | tf_op | source)
XLA Modules:
  0.0 295.8 jit_solution(7449189479999272801)
XLA Ops:
  0.6 0.0 copy-start
  0.6 0.0 copy-start.3
  0.7 1.7 collective-permute-start.1
  2.3 1.1 copy.17
  3.4 1.9 collective-permute-start
  5.3 28.4 %collective-permute-done = bf16[1,128,1024]{1,2,0:T(8,128)(2,1)S(1)} collective-permute-done((bf16[1,128,1024]{1,2,0:T(8,128)(2,1)S(1)}, bf16[1,128,1024]{1,2,0:T(8,128)(2,1)S(1)}, u32[]{:S(2)}, u32[]{:S(2)}) %collective-permute-start) | collective-permute-done | bytes 262176 | tf_op jit(solution)/shard_map/ppermute | solution.py:46
  33.8 0.1 pad_maximum_fusion
  33.8 1.0 copy.19
  34.8 3.5 %all-to-all-start = ((bf16[2,2,1,256,256]{4,3,0,2,1:T(8,128)(2,1)}), bf16[2,2,1,256,256]{4,3,0,2,1:T(8,128)(2,1)S(1)}, u32[]{:S(2)}, u32[]{:S(2)}) async-start(bf16[2,2,1,256,256]{4,3,0,2,1:T(8,128)(2,1)} %copy.19), calls=%async_computation | async-start | bytes 1048576 | tf_op jit(solution)/shard_map/all_to_all | solution.py:33
  38.3 0.0 collective-permute-done.1
  38.3 0.0 copy-done.3
  38.4 2.5 maximum_bitcast_fusion
  40.9 0.0 all-to-all-done
  40.9 5.0 %stack.2 = bf16[4,1,256,3584]{3,2,1,0:T(8,128)(2,1)} broadcast(bf16[256,3584]{1,0:T(8,128)(2,1)} %maximum_bitcast_fusion), dimensions={2,3} | broadcast | bytes 9175040 | tf_op jit(solution)/shard_map/stack | solution.py:13
  45.9 0.0 copy-start.5
  45.9 5.6 %all-to-all-start.2 = ((bf16[4,1,256,3584]{3,2,1,0:T(8,128)(2,1)}), bf16[4,1,256,3584]{3,2,1,0:T(8,128)(2,1)}, u32[]{:S(2)}, u32[]{:S(2)}) async-start(bf16[4,1,256,3584]{3,2,1,0:T(8,128)(2,1)} %stack.2), calls=%async_computation.2 | async-start | bytes 14680064 | tf_op jit(solution)/shard_map/all_to_all | solution.py:14
  51.5 0.0 copy-done.5
  51.5 0.2 fusion.18
  51.7 0.8 dynamic-slice_select_fusion.1
  52.5 0.8 copy.20
  53.4 81.5 %all-to-all-done.2 = bf16[4,1,256,3584]{3,2,1,0:T(8,128)(2,1)} async-done(((bf16[4,1,256,3584]{3,2,1,0:T(8,128)(2,1)}), bf16[4,1,256,3584]{3,2,1,0:T(8,128)(2,1)}, u32[]{:S(2)}, u32[]{:S(2)}) %all-to-all-start.2) | async-done | bytes 7340064 | tf_op jit(solution)/shard_map/all_to_all | solution.py:14
  134.9 3.5 %all-to-all-start.1 = ((bf16[2,2,1,256,256]{4,3,1,2,0:T(8,128)(2,1)}), bf16[2,2,1,256,256]{4,3,1,2,0:T(8,128)(2,1)S(1)}, u32[]{:S(2)}, u32[]{:S(2)}) async-start(bf16[2,2,1,256,256]{4,3,1,2,0:T(8,128)(2,1)} %copy.20), calls=%async_computation.1 | async-start | bytes 1048576 | tf_op jit(solution)/shard_map/all_to_all | solution.py:33
  138.4 6.6 %fusion.6 = f32[1024,256]{1,0:T(8,128)} fusion(bf16[1024,3584]{1,0:T(8,128)(2,1)} %bitcast.5, bf16[1,3584,256]{2,1,0:T(8,128)(2,1)} %param.20), kind=kOutput, calls=%fused_computation.10 | convolution fusion | flops 1879048192 | bytes 10223616 | tf_op jit(solution)/shard_map/dot_general | solution.py:73
  145.0 2.8 all-to-all-done.1
  147.8 0.0 copy-start.4
  147.8 0.8 copy-done.4
  148.6 0.0 copy-done
  148.6 0.0 copy-start.2
  148.6 5.9 %multiply_convert_fusion = (bf16[1024,256]{1,0:T(8,128)(2,1)S(1)}, bf16[1024,256]{1,0:T(8,128)(2,1)S(1)}, bf16[1024,256]{1,0:T(8,128)(2,1)S(1)}) fusion(f32[1024]{0:T(1024)S(1)} %bitcast.50, f32[1024,256]{1,0:T(8,128)} %fusion.6, bf16[2,2,1,256,256]{4,3,1,2,0:T(8,128)(2,1)} %copy-done.4, bf16[1024,3584]{1,0:T(8,128)(2,1)} %bitcast.5, ...), kind=kOutput, calls=%fused_computation.23 | convolution fusion | flops 1883766784 | bytes 12324864 | tf_op jit(solution)/shard_map/dot_general | solution.py:74
  154.6 0.0 copy-done.2
  154.6 7.3 %fusion.4 = f32[1024,3584]{1,0:T(8,128)} fusion(bf16[1024,256]{1,0:T(8,128)(2,1)S(1)} %get-tuple-element.48, bf16[1,3584,256]{2,1,0:T(8,128)(2,1)S(1)} %copy-done.2), kind=kOutput, calls=%fused_computation.8 | convolution fusion | flops 1879048192 | bytes 17039360 | tf_op jit(solution)/shard_map/dot_general | solution.py:56
  161.9 10.2 %add_convert_fusion = bf16[1024,3584]{1,0:T(8,128)(2,1)} fusion(f32[1024,3584]{1,0:T(8,128)} %fusion.4, bf16[1024,256]{1,0:T(8,128)(2,1)S(1)} %get-tuple-element.49, bf16[1,3584,256]{2,1,0:T(8,128)(2,1)S(1)} %copy-done), kind=kOutput, calls=%fused_computation | convolution fusion | flops 1886388224 | bytes 24379392 | tf_op jit(solution)/shard_map/dot_general | solution.py:56
  172.1 5.4 %all-to-all-start.3 = ((bf16[4,1,256,3584]{3,2,1,0:T(8,128)(2,1)}), bf16[4,1,256,3584]{3,2,1,0:T(8,128)(2,1)}, u32[]{:S(2)}, u32[]{:S(2)}) async-start(bf16[4,1,256,3584]{3,2,1,0:T(8,128)(2,1)} %bitcast.44), calls=%async_computation.3 | async-start | bytes 14680064 | tf_op jit(solution)/shard_map/all_to_all | solution.py:51
  177.6 0.7 slice.47
  178.3 1.7 collective-permute-start.3
  180.0 6.4 %fusion.3 = bf16[1,3584,256]{2,1,0:T(8,128)(2,1)} fusion(bf16[1024,3584]{1,0:T(8,128)(2,1)} %bitcast.5, bf16[1024,256]{1,0:T(8,128)(2,1)S(1)} %get-tuple-element.48), kind=kOutput, calls=%fused_computation.6 | convolution fusion | flops 1880883200 | bytes 9699328 | tf_op jit(solution)/shard_map/dot_general | solution.py:56
  186.5 78.5 %all-to-all-done.3 = bf16[4,1,256,3584]{3,2,1,0:T(8,128)(2,1)} async-done(((bf16[4,1,256,3584]{3,2,1,0:T(8,128)(2,1)}), bf16[4,1,256,3584]{3,2,1,0:T(8,128)(2,1)}, u32[]{:S(2)}, u32[]{:S(2)}) %all-to-all-start.3) | async-done | bytes 7340064 | tf_op jit(solution)/shard_map/all_to_all | solution.py:51
  265.0 6.0 %reduce_sum.14 = bf16[256,3584]{1,0:T(8,128)(2,1)} reduce(bf16[4,1,256,3584]{3,2,1,0:T(8,128)(2,1)} %all-to-all-done.3, bf16[]{:T(256)} %constant.151.clone.1), dimensions={0,1}, to_apply=%region_0.2 | reduce | flops 2752512 | bytes 9175042 | tf_op jit(solution)/shard_map/reduce_sum | solution.py:52
  271.0 1.2 slice.45
  272.3 0.0 copy-start.1
  272.3 0.1 collective-permute-start.2
  272.4 6.6 %fusion.2 = bf16[1,3584,256]{2,1,0:T(8,128)(2,1)} fusion(bf16[1024,3584]{1,0:T(8,128)(2,1)} %bitcast.5, bf16[1024,256]{1,0:T(8,128)(2,1)S(1)} %get-tuple-element.49), kind=kOutput, calls=%fused_computation.5 | convolution fusion | flops 1880883200 | bytes 9699328 | tf_op jit(solution)/shard_map/dot_general | solution.py:56
  278.9 0.0 collective-permute-done.3
  278.9 1.7 add_convert_fusion.2
  280.7 14.0 %collective-permute-done.2 = bf16[1,128,3584]{2,1,0:T(8,128)(2,1)S(1)} collective-permute-done((bf16[1,128,3584]{2,1,0:T(8,128)(2,1)S(1)}, bf16[1,128,3584]{2,1,0:T(8,128)(2,1)S(1)}, u32[]{:S(2)}, u32[]{:S(2)}) %collective-permute-start.2) | collective-permute-done | bytes 917536 | tf_op jit(solution)/shard_map/ppermute | solution.py:46
  294.7 0.0 copy-done.1
  294.7 1.1 add_convert_fusion.1
  (2 shorter events, 0.0 us)
Async XLA Ops:
  0.6 148.0 %copy-start = (bf16[1,3584,256]{2,1,0:T(8,128)(2,1)S(1)}, bf16[1,3584,256]{2,1,0:T(8,128)(2,1)}, u32[]{:S(2)}) copy-start(bf16[1,3584,256]{2,1,0:T(8,128)(2,1)} %param.21) | copy-start | bytes 5505028
  0.6 37.7 %copy-start.3 = (bf16[1,128,3584]{2,1,0:T(8,128)(2,1)S(1)}, bf16[1,128,3584]{2,1,0:T(8,128)(2,1)}, u32[]{:S(2)}) copy-start(bf16[1,128,3584]{2,1,0:T(8,128)(2,1)} %param.16) | copy-start | bytes 2752516
  0.7 37.7 %collective-permute-start.1 = (bf16[1,128,3584]{2,1,0:T(8,128)(2,1)}, bf16[1,128,3584]{2,1,0:T(8,128)(2,1)}, u32[]{:S(2)}, u32[]{:S(2)}) collective-permute-start(bf16[1,128,3584]{2,1,0:T(8,128)(2,1)} %param.16), channel_id=1, source_target_pairs={{0,1},{1,2},{2,3},{3,4},{4,5},{5,6},{6,7},{7,8},{8,9},{9,10},{10,1... | collective-permute-start | bytes 2752520 | tf_op jit(solution)/shard_map/ppermute | solution.py:46
  3.4 30.3 %collective-permute-start = (bf16[1,128,1024]{1,2,0:T(8,128)(2,1)S(1)}, bf16[1,128,1024]{1,2,0:T(8,128)(2,1)S(1)}, u32[]{:S(2)}, u32[]{:S(2)}) collective-permute-start(bf16[1,128,1024]{1,2,0:T(8,128)(2,1)S(1)} %copy.17), channel_id=1, source_target_pairs={{0,1},{1,2},{2,3},{3,4},{4,5},{5,6},{6,7},{7,8},{8,9},{9,10},{10,1... | collective-permute-start | bytes 786440 | tf_op jit(solution)/shard_map/ppermute | solution.py:46
  34.8 6.0 %all-to-all-start = ((bf16[2,2,1,256,256]{4,3,0,2,1:T(8,128)(2,1)}), bf16[2,2,1,256,256]{4,3,0,2,1:T(8,128)(2,1)S(1)}, u32[]{:S(2)}, u32[]{:S(2)}) async-start(bf16[2,2,1,256,256]{4,3,0,2,1:T(8,128)(2,1)} %copy.19), calls=%async_computation | async-start | bytes 1048576 | tf_op jit(solution)/shard_map/all_to_all | solution.py:33
  45.9 5.6 %copy-start.5 = (s32[4,64]{1,0:T(4,128)S(1)}, s32[4,64]{1,0:T(4,128)}, u32[]{:S(2)}) copy-start(s32[4,64]{1,0:T(4,128)} %param.19) | copy-start | bytes 3076
  45.9 89.0 %all-to-all-start.2 = ((bf16[4,1,256,3584]{3,2,1,0:T(8,128)(2,1)}), bf16[4,1,256,3584]{3,2,1,0:T(8,128)(2,1)}, u32[]{:S(2)}, u32[]{:S(2)}) async-start(bf16[4,1,256,3584]{3,2,1,0:T(8,128)(2,1)} %stack.2), calls=%async_computation.2 | async-start | bytes 14680064 | tf_op jit(solution)/shard_map/all_to_all | solution.py:14
  134.9 12.9 %all-to-all-start.1 = ((bf16[2,2,1,256,256]{4,3,1,2,0:T(8,128)(2,1)}), bf16[2,2,1,256,256]{4,3,1,2,0:T(8,128)(2,1)S(1)}, u32[]{:S(2)}, u32[]{:S(2)}) async-start(bf16[2,2,1,256,256]{4,3,1,2,0:T(8,128)(2,1)} %copy.20), calls=%async_computation.1 | async-start | bytes 1048576 | tf_op jit(solution)/shard_map/all_to_all | solution.py:33
  147.8 0.8 copy-start.4
  148.6 5.9 %copy-start.2 = (bf16[1,3584,256]{2,1,0:T(8,128)(2,1)S(1)}, bf16[1,3584,256]{2,1,0:T(8,128)(2,1)}, u32[]{:S(2)}) copy-start(bf16[1,3584,256]{2,1,0:T(8,128)(2,1)} %param.20) | copy-start | bytes 5505028
  172.1 92.9 %all-to-all-start.3 = ((bf16[4,1,256,3584]{3,2,1,0:T(8,128)(2,1)}), bf16[4,1,256,3584]{3,2,1,0:T(8,128)(2,1)}, u32[]{:S(2)}, u32[]{:S(2)}) async-start(bf16[4,1,256,3584]{3,2,1,0:T(8,128)(2,1)} %bitcast.44), calls=%async_computation.3 | async-start | bytes 14680064 | tf_op jit(solution)/shard_map/all_to_all | solution.py:51
  178.3 100.6 %collective-permute-start.3 = (bf16[4,128,256]{2,1,0:T(8,128)(2,1)}, bf16[4,128,256]{2,1,0:T(8,128)(2,1)}, u32[]{:S(2)}, u32[]{:S(2)}) collective-permute-start(bf16[4,128,256]{2,1,0:T(8,128)(2,1)} %slice.47), channel_id=1, source_target_pairs={{0,63},{1,0},{2,1},{3,2},{4,3},{5,4},{6,5},{7,6},{8,7},{9,8},{10,9... | collective-permute-start | bytes 786440 | tf_op jit(solution)/shard_map/ppermute | solution.py:46
  272.3 22.4 %copy-start.1 = (bf16[256,3584]{1,0:T(8,128)(2,1)S(1)}, bf16[256,3584]{1,0:T(8,128)(2,1)}, u32[]{:S(2)}) copy-start(bf16[256,3584]{1,0:T(8,128)(2,1)} %reduce_sum.14) | copy-start | bytes 5505028
  272.3 22.4 %collective-permute-start.2 = (bf16[1,128,3584]{2,1,0:T(8,128)(2,1)S(1)}, bf16[1,128,3584]{2,1,0:T(8,128)(2,1)S(1)}, u32[]{:S(2)}, u32[]{:S(2)}) collective-permute-start(bf16[1,128,3584]{2,1,0:T(8,128)(2,1)S(1)} %slice.45), channel_id=1, source_target_pairs={{0,63},{1,0},{2,1},{3,2},{4,3},{5,4},{6,5},{7,6},{8,7},{9,8},{10,9... | collective-permute-start | bytes 2752520 | tf_op jit(solution)/shard_map/ppermute | solution.py:46
